TPU v7x, 32 devices: a whole 2x2x4 slice. The times are simulated.
32 devices in a mesh: row: 4 (over y, core), col: 4 (over z), lag: 2 (over x).
Axes of the slice: x: 2, y: 2, z: 4, core: 2. Of those that a mesh axis runs over, the one named last changes fastest.
Arguments:
- trajectories: bfloat16 [4096, 4096], P(('row', 'col'), 'lag'), may hold values from -6 to 6
- pair_live: int32 [4, 4], replicated, may hold values from 0 to 1, as said below
Outputs:
- gram: bfloat16 [4096, 4096], P(('row', 'lag'), 'col')
Inputs may be any that keep to these rules, and one draw needn't show every extreme that they name: `pair_live`: Symmetric, with every diagonal entry 1.
All inputs are finite; a program needn't handle non-finite values.
Results may differ from a plain program's by a relative error of at most 0.0015.
Values may be sent and summed in bfloat16 or wider, within the bound.
A program may use at most 64 MiB of HBM per device.

v0:
```python
import functools

import jax
import jax.numpy as jnp
from jax import lax
from jax.experimental import pallas as pl
from jax.experimental.pallas import tpu as pltpu
from jax.sharding import PartitionSpec as P

MESH = pl.DeviceIdType.MESH
SPLIT = 2
SUB = 1
NT_DIMS = (((1,), (1,)), ((), ()))


def kernel(
    rows, cols, lags, split, samples,
    x_ref, live_ref, out_ref,
    rb, rn, cn, tile, got,
    own_sem, z_send, z_recv, c_send, c_recv, t_send, t_recv,
):
    r, c, l = lax.axis_index("row"), lax.axis_index("col"), lax.axis_index("lag")
    units = cols * split
    m = rb.shape[1]
    mine = units // lags
    bits = rows.bit_length() - 1
    node = lax.bitwise_xor(r, c)
    base = jnp.where(node == 0, 0, units)

    own = pltpu.make_async_copy(
        x_ref, rb.at[pl.ds(c * split, split)], own_sem
    )
    own.start()

    barrier = pltpu.get_barrier_semaphore()
    for j in range(1, rows):
        pl.semaphore_signal(
            barrier, device_id={"row": lax.rem(r + j, rows)}, device_id_type=MESH
        )
    for j in range(1, lags):
        pl.semaphore_signal(
            barrier, device_id={"lag": lax.rem(l + j, lags)}, device_id_type=MESH
        )

    @pl.when(c > 0)
    def _():
        pl.semaphore_signal(barrier, device_id={"col": c - 1}, device_id_type=MESH)

    @pl.when(c < cols - 1)
    def _():
        pl.semaphore_signal(barrier, device_id={"col": c + 1}, device_id_type=MESH)

    beside = jnp.where(jnp.logical_or(c == 0, c == cols - 1), 1, 2)
    pl.semaphore_wait(barrier, rows - 1 + lags - 1 + beside)
    own.wait()

    chunk = m // SUB

    def part(ref, u, h):
        return ref.at[u, pl.ds(h * chunk, chunk)]

    def along(side, u, h):
        to = jnp.clip(c + 1 - 2 * side, 0, cols - 1)
        return pltpu.make_async_remote_copy(
            part(rb, u, h), part(rb, u, h), z_send.at[side, u, h], z_recv.at[u, h],
            device_id={"col": to}, device_id_type=MESH,
        )

    def down(bit, u, h):
        return pltpu.make_async_remote_copy(
            part(rb, base + u, h), part(rb, units + u, h), c_send.at[bit, u, h], c_recv.at[u, h],
            device_id={"row": lax.bitwise_xor(r, 1 << bit)}, device_id_type=MESH,
        )

    def has_child(bit):
        return lax.rem(node, 2 << bit) == 0

    def across(i, j):
        owner = i // mine
        hop = lax.rem(owner - l + lags, lags)
        slot = jnp.maximum(hop - 1, 0)
        return pltpu.make_async_remote_copy(
            tile.at[i, j], got.at[slot, lax.rem(i, mine), j],
            t_send.at[i, j], t_recv.at[slot, lax.rem(i, mine), j],
            device_id={"lag": owner}, device_id_type=MESH,
        )

    def valid(side, d):
        k = c - d if side == 0 else c + d
        return jnp.logical_and(k >= 0, k < cols), k

    def goes_on(side):
        return c < cols - 1 if side == 0 else c > 0

    half = cols // lags
    final = (cols - 1) * split - 1

    def is_late(where, lag):
        if split == 1 or cols < 3:
            return False
        return jnp.logical_or(
            jnp.logical_and(where == 0, 1 // half == lag),
            jnp.logical_and(where == cols - 1, (cols - 2) // half == lag),
        )

    def arrival(q):
        p = q - split
        moved = jnp.where(p == final, split - 1, jnp.where(p >= split - 1, p + 1, p))
        return jnp.where(jnp.logical_and(is_late(c, l), p >= 0), split + moved, q)

    def last_unit(lag):
        far = jnp.where(2 * c < cols, cols - 1, 0)
        near = jnp.where(c == 0, 1, cols - 2)
        return jnp.where(is_late(c, lag), near, far) * split + split - 1

    def holds_back(side):
        if split == 1 or cols < 3:
            return False
        to = c + 1 - 2 * side
        return jnp.logical_and(to == (cols - 1 if side == 0 else 0), is_late(to, l))

    def unit_at(q, side):
        e = arrival(q)
        d = e // split
        ok, k = valid(side, d)
        u = jnp.clip(k, 0, cols - 1) * split + e - d * split
        return ok, jnp.logical_and(ok, jnp.logical_or(d > 0, side == 0)), u

    def one_round(q, carry):
        d = arrival(q) // split
        here = [unit_at(q, side) for side in range(2)]

        def unit(side):
            return here[side]

        def one_chunk(h, carry):
            for side in range(2):
                ok, first, u = unit(side)

                @pl.when(jnp.logical_and(ok, d > 0))
                def _():
                    along(side, u, h).wait_recv()

                held_back = jnp.logical_and(holds_back(side), q == split - 1)

                @pl.when(
                    jnp.logical_and(
                        jnp.logical_and(ok, goes_on(side)), jnp.logical_not(held_back)
                    )
                )
                def _():
                    along(side, u, h).start()

                @pl.when(jnp.logical_and(holds_back(side), q == final))
                def _():
                    along(side, c * split + split - 1, h).start()

                @pl.when(jnp.logical_and(first, node == 0))
                def _():
                    for bit in reversed(range(bits)):
                        down(bit, u, h).start()

            for side in range(2):
                ok, first, u = unit(side)

                @pl.when(jnp.logical_and(first, node != 0))
                def _():
                    down(0, u, h).wait_recv()
                    for bit in reversed(range(bits)):

                        @pl.when(has_child(bit))
                        def _():
                            down(bit, u, h).start()

            return carry

        lax.fori_loop(0, SUB, one_chunk, 0)

        for side in range(2):
            ok, first, u = unit(side)

            @pl.when(first)
            def _():
                a = rb[u].astype(jnp.float32)
                rn[u] = jnp.broadcast_to(
                    jnp.sum(a * a, axis=1, keepdims=True), rn.shape[1:]
                )
                b = rb[base + u].astype(jnp.float32)
                n = jnp.broadcast_to(jnp.sum(b * b, axis=1, keepdims=True), (m, 128))
                cn[u] = n.T[:8]

        def one_tile(i, j, leaves):
            @pl.when((i // mine != l) == leaves)
            def _():
                inner = lax.dot_general(
                    rb[i], rb[base + j], NT_DIMS, preferred_element_type=jnp.float32
                )
                tile[i, j] = rn[i][:, :1] + cn[j][:1] - 2.0 * inner
                if leaves:
                    across(i, j).start()

        def pairs(leaves, p, carry):
            q2, side2 = p // 2, lax.rem(p, 2)
            e = arrival(q2)
            d2 = e // split
            k = c + jnp.where(side2 == 0, -d2, d2)
            found = jnp.logical_and(k >= 0, k < cols)
            found = jnp.logical_and(found, jnp.logical_or(d2 > 0, side2 == 0))
            v = jnp.clip(k, 0, cols - 1) * split + e - d2 * split
            for side in range(2):
                _, first, u = unit(side)

                @pl.when(jnp.logical_and(first, found))
                def _():
                    one_tile(u, v, leaves)

                    @pl.when(q2 < q)
                    def _():
                        one_tile(v, u, leaves)

            return carry

        for leaves in (True, False):
            lax.fori_loop(0, 2 * q + 2, functools.partial(pairs, leaves), 0)
        return carry

    lax.fori_loop(0, units, one_round, 0)

    live = live_ref[r, c].astype(jnp.float32)

    def finish(last, kk, carry):
        i = l * mine + kk
        for j in range(units):
            comes_last = False
            for o in range(1, lags):
                end = last_unit(lax.rem(l + o, lags))
                comes_last = jnp.logical_or(
                    comes_last, jnp.logical_or(i == end, j == end)
                )

            @pl.when(comes_last == last)
            def _():
                total = tile[i, j]
                for o in range(lags - 1):
                    pltpu.make_async_remote_copy(
                        tile.at[i, j], got.at[o, kk, j], t_send.at[i, j],
                        t_recv.at[o, kk, j],
                        device_id={"lag": lax.rem(l + 1, lags)},
                        device_id_type=MESH,
                    ).wait_recv()
                    total = total + got[o, kk, j]
                gram = jnp.exp(-2.0 * total / samples) * live
                out_ref[pl.ds(kk * m, m), j * m : (j + 1) * m] = gram.astype(
                    out_ref.dtype
                )

        return carry

    for last in (False, True):
        lax.fori_loop(0, mine, functools.partial(finish, last), 0)

    def drain(u, carry):
        k = u // split
        for h in range(SUB):

            @pl.when(jnp.logical_and(k <= c, c < cols - 1))
            def _():
                along(0, u, h).wait_send()

            @pl.when(jnp.logical_and(k >= c, c > 0))
            def _():
                along(1, u, h).wait_send()

            for bit in range(bits):

                @pl.when(has_child(bit))
                def _():
                    down(bit, u, h).wait_send()

        @pl.when(u // mine != l)
        def _():
            def each(j, carry):
                across(u, j).wait_send()
                return carry

            lax.fori_loop(0, units, each, 0)

        return carry

    lax.fori_loop(0, units, drain, 0)


def on_device(rows, cols, lags, trajectories, pair_live):
    held, width = trajectories.shape
    split = SPLIT if held % (SPLIT * 128) == 0 else 1
    m = held // split
    units = cols * split
    mine = units // lags
    bits = rows.bit_length() - 1
    dma = pltpu.SemaphoreType.DMA
    return pl.pallas_call(
        functools.partial(kernel, rows, cols, lags, split, width * lags),
        out_shape=jax.ShapeDtypeStruct((mine * m, units * m), jnp.bfloat16),
        in_specs=[
            pl.BlockSpec(memory_space=pl.ANY),
            pl.BlockSpec(memory_space=pltpu.SMEM),
        ],
        out_specs=pl.BlockSpec(memory_space=pltpu.VMEM),
        scratch_shapes=[
            pltpu.VMEM((2 * units, m, width), jnp.bfloat16),
            pltpu.VMEM((units, m, 128), jnp.float32),
            pltpu.VMEM((units, 8, m), jnp.float32),
            pltpu.VMEM((units, units, m, m), jnp.float32),
            pltpu.VMEM((lags - 1, mine, units, m, m), jnp.float32),
            dma,
            dma((2, units, SUB)),
            dma((units, SUB)),
            dma((bits, units, SUB)),
            dma((units, SUB)),
            dma((units, units)),
            dma((lags - 1, mine, units)),
        ],
        compiler_params=pltpu.CompilerParams(
            collective_id=0, has_side_effects=True, vmem_limit_bytes=60 * 2**20
        ),
    )(trajectories.reshape(split, m, width), pair_live)


def solution(mesh):
    size = mesh.shape
    return jax.shard_map(
        functools.partial(on_device, size["row"], size["col"], size["lag"]),
        mesh=mesh,
        in_specs=(P(("row", "col"), "lag"), P()),
        out_specs=P(("row", "lag"), "col"),
        check_vma=False,
    )
```

profile of v0, /device:TPU:24, one launch (start us, length us, event | category | flops | bytes accessed | tf_op | source)
XLA Modules:
  0.0 102.4 jit_solution(1295015426390058179)
XLA Ops:
  0.0 100.2 %shard_map.28 = bf16[512,1024]{1,0:T(8,128)(2,1)} custom-call(bf16[2,128,2048]{2,1,0:T(8,128)(2,1)} %bitcast.1, s32[4,4]{1,0:T(4,128)} %live_ref.1), custom_call_target="tpu_custom_call" | custom-call | tf_op jit(solution)/shard_map/pallas_call | solution.py:301
  100.2 2.3 %copy.4 = bf16[512,1024]{1,0:T(8,128)(2,1)} copy(bf16[512,1024]{1,0:T(8,128)(2,1)} %shard_map.28) | data formatting | bytes 2097152
where the time goes:
time: 103 us; the launch traced here: 102 us
  Pallas kernels  100 us (97%)
  local copies, waits for them, and re-layouts  2.26 us (2%)
    pallas_call x1, Pallas kernels, on_device(): pl.pallas_call(functools.partial(kernel, rows, cols, lags, split, width *...  100 us
    unnamed x1, local copies, waits for them, and re-layouts  2.26 us

commit v1 on v0

--- a/solution.py
+++ b/solution.py
@@ -16,8 +16,8 @@
 def kernel(
     rows, cols, lags, split, samples,
     x_ref, live_ref, out_ref,
-    rb, rn, cn, tile, got,
-    own_sem, z_send, z_recv, c_send, c_recv, t_send, t_recv,
+    rb, rn, cn, tile, got, turned, given,
+    own_sem, z_send, z_recv, c_send, c_recv, t_send, t_recv, m_send, m_recv,
 ):
     r, c, l = lax.axis_index("row"), lax.axis_index("col"), lax.axis_index("lag")
     units = cols * split
@@ -26,6 +26,12 @@
     bits = rows.bit_length() - 1
     node = lax.bitwise_xor(r, c)
     base = jnp.where(node == 0, 0, units)
+    at_end = jnp.logical_or(c == 0, c == cols - 1)
+    inside = jnp.logical_and(r > 0, r < rows - 1)
+    lo = jnp.where(inside, 1, 0)
+    hi = jnp.where(inside, cols - 2, cols - 1)
+    computes = jnp.logical_not(jnp.logical_and(inside, at_end))
+    mirrors = jnp.logical_not(jnp.logical_or(inside, at_end))
 
     own = pltpu.make_async_copy(
         x_ref, rb.at[pl.ds(c * split, split)], own_sem
@@ -50,7 +56,16 @@
     def _():
         pl.semaphore_signal(barrier, device_id={"col": c + 1}, device_id_type=MESH)
 
-    beside = jnp.where(jnp.logical_or(c == 0, c == cols - 1), 1, 2)
+    paired = jnp.logical_or(mirrors, jnp.logical_not(computes))
+
+    @pl.when(paired)
+    def _():
+        for o in range(lags):
+            pl.semaphore_signal(
+                barrier, device_id={"row": c, "col": r, "lag": o}, device_id_type=MESH
+            )
+
+    beside = jnp.where(at_end, 1, 2) + jnp.where(paired, lags, 0)
     pl.semaphore_wait(barrier, rows - 1 + lags - 1 + beside)
     own.wait()
 
@@ -90,44 +105,19 @@
         return jnp.logical_and(k >= 0, k < cols), k
 
     def goes_on(side):
-        return c < cols - 1 if side == 0 else c > 0
-
-    half = cols // lags
-    final = (cols - 1) * split - 1
-
-    def is_late(where, lag):
-        if split == 1 or cols < 3:
-            return False
-        return jnp.logical_or(
-            jnp.logical_and(where == 0, 1 // half == lag),
-            jnp.logical_and(where == cols - 1, (cols - 2) // half == lag),
-        )
-
-    def arrival(q):
-        p = q - split
-        moved = jnp.where(p == final, split - 1, jnp.where(p >= split - 1, p + 1, p))
-        return jnp.where(jnp.logical_and(is_late(c, l), p >= 0), split + moved, q)
-
-    def last_unit(lag):
-        far = jnp.where(2 * c < cols, cols - 1, 0)
-        near = jnp.where(c == 0, 1, cols - 2)
-        return jnp.where(is_late(c, lag), near, far) * split + split - 1
-
-    def holds_back(side):
-        if split == 1 or cols < 3:
-            return False
-        to = c + 1 - 2 * side
-        return jnp.logical_and(to == (cols - 1 if side == 0 else 0), is_late(to, l))
+        return c < hi if side == 0 else c > lo
+
+    def last_unit():
+        return jnp.where(2 * c < cols, cols - 1, 0) * split + split - 1
 
     def unit_at(q, side):
-        e = arrival(q)
-        d = e // split
+        d = q // split
         ok, k = valid(side, d)
-        u = jnp.clip(k, 0, cols - 1) * split + e - d * split
+        u = jnp.clip(k, 0, cols - 1) * split + q - d * split
         return ok, jnp.logical_and(ok, jnp.logical_or(d > 0, side == 0)), u
 
     def one_round(q, carry):
-        d = arrival(q) // split
+        d = q // split
         here = [unit_at(q, side) for side in range(2)]
 
         def unit(side):
@@ -137,23 +127,15 @@
             for side in range(2):
                 ok, first, u = unit(side)
 
+                ok = jnp.logical_and(ok, jnp.logical_or(d == 0, computes))
+
                 @pl.when(jnp.logical_and(ok, d > 0))
                 def _():
                     along(side, u, h).wait_recv()
 
-                held_back = jnp.logical_and(holds_back(side), q == split - 1)
-
-                @pl.when(
-                    jnp.logical_and(
-                        jnp.logical_and(ok, goes_on(side)), jnp.logical_not(held_back)
-                    )
-                )
+                @pl.when(jnp.logical_and(ok, goes_on(side)))
                 def _():
                     along(side, u, h).start()
-
-                @pl.when(jnp.logical_and(holds_back(side), q == final))
-                def _():
-                    along(side, c * split + split - 1, h).start()
 
                 @pl.when(jnp.logical_and(first, node == 0))
                 def _():
@@ -179,7 +161,7 @@
         for side in range(2):
             ok, first, u = unit(side)
 
-            @pl.when(first)
+            @pl.when(jnp.logical_and(first, computes))
             def _():
                 a = rb[u].astype(jnp.float32)
                 rn[u] = jnp.broadcast_to(
@@ -201,12 +183,11 @@
 
         def pairs(leaves, p, carry):
             q2, side2 = p // 2, lax.rem(p, 2)
-            e = arrival(q2)
-            d2 = e // split
+            d2 = q2 // split
             k = c + jnp.where(side2 == 0, -d2, d2)
             found = jnp.logical_and(k >= 0, k < cols)
             found = jnp.logical_and(found, jnp.logical_or(d2 > 0, side2 == 0))
-            v = jnp.clip(k, 0, cols - 1) * split + e - d2 * split
+            v = jnp.clip(k, 0, cols - 1) * split + q2 - d2 * split
             for side in range(2):
                 _, first, u = unit(side)
 
@@ -220,23 +201,30 @@
 
             return carry
 
-        for leaves in (True, False):
-            lax.fori_loop(0, 2 * q + 2, functools.partial(pairs, leaves), 0)
+        @pl.when(computes)
+        def _():
+            for leaves in (True, False):
+                lax.fori_loop(0, 2 * q + 2, functools.partial(pairs, leaves), 0)
+
         return carry
 
     lax.fori_loop(0, units, one_round, 0)
 
     live = live_ref[r, c].astype(jnp.float32)
+    end = last_unit()
+
+    def mirror(kk, j):
+        return pltpu.make_async_remote_copy(
+            turned.at[kk, j],
+            given.at[j % mine, l * mine + kk],
+            m_send.at[kk, j], m_recv.at[j % mine, l * mine + kk],
+            device_id={"row": c, "col": r, "lag": j // mine}, device_id_type=MESH,
+        )
 
     def finish(last, kk, carry):
         i = l * mine + kk
         for j in range(units):
-            comes_last = False
-            for o in range(1, lags):
-                end = last_unit(lax.rem(l + o, lags))
-                comes_last = jnp.logical_or(
-                    comes_last, jnp.logical_or(i == end, j == end)
-                )
+            comes_last = jnp.logical_or(i == end, j == end)
 
             @pl.when(comes_last == last)
             def _():
@@ -254,20 +242,54 @@
                     out_ref.dtype
                 )
 
+                @pl.when(mirrors)
+                def _():
+                    turned[kk, j] = gram.T.astype(out_ref.dtype)
+                    mirror(kk, j).start()
+
         return carry
 
-    for last in (False, True):
-        lax.fori_loop(0, mine, functools.partial(finish, last), 0)
+    @pl.when(computes)
+    def _():
+        for last in (False, True):
+            lax.fori_loop(0, mine, functools.partial(finish, last), 0)
+
+    @pl.when(mirrors)
+    def _():
+        def sent(kk, carry):
+            for j in range(units):
+                mirror(kk, j).wait_send()
+            return carry
+
+        lax.fori_loop(0, mine, sent, 0)
+
+    @pl.when(jnp.logical_not(computes))
+    def _():
+        def landed(kk, carry):
+            for i in range(units):
+                pltpu.make_async_remote_copy(
+                    turned.at[0, 0],
+                    given.at[kk, i],
+                    m_send.at[0, 0], m_recv.at[kk, i],
+                    device_id={"row": c, "col": r, "lag": i // mine},
+                    device_id_type=MESH,
+                ).wait_recv()
+                out_ref[pl.ds(kk * m, m), i * m : (i + 1) * m] = given[kk, i]
+            return carry
+
+        lax.fori_loop(0, mine, landed, 0)
 
     def drain(u, carry):
         k = u // split
         for h in range(SUB):
 
-            @pl.when(jnp.logical_and(k <= c, c < cols - 1))
+            got_it = jnp.logical_or(k == c, computes)
+
+            @pl.when(jnp.logical_and(got_it, jnp.logical_and(k <= c, goes_on(0))))
             def _():
                 along(0, u, h).wait_send()
 
-            @pl.when(jnp.logical_and(k >= c, c > 0))
+            @pl.when(jnp.logical_and(got_it, jnp.logical_and(k >= c, goes_on(1))))
             def _():
                 along(1, u, h).wait_send()
 
@@ -277,7 +299,7 @@
                 def _():
                     down(bit, u, h).wait_send()
 
-        @pl.when(u // mine != l)
+        @pl.when(jnp.logical_and(u // mine != l, computes))
         def _():
             def each(j, carry):
                 across(u, j).wait_send()
@@ -312,6 +334,8 @@
             pltpu.VMEM((units, 8, m), jnp.float32),
             pltpu.VMEM((units, units, m, m), jnp.float32),
             pltpu.VMEM((lags - 1, mine, units, m, m), jnp.float32),
+            pltpu.VMEM((mine, units, m, m), jnp.bfloat16),
+            pltpu.VMEM((mine, units, m, m), jnp.bfloat16),
             dma,
             dma((2, units, SUB)),
             dma((units, SUB)),
@@ -319,6 +343,8 @@
             dma((units, SUB)),
             dma((units, units)),
             dma((lags - 1, mine, units)),
+            dma((mine, units)),
+            dma((mine, units)),
         ],
         compiler_params=pltpu.CompilerParams(
             collective_id=0, has_side_effects=True, vmem_limit_bytes=60 * 2**20

time: 103 us -> 96.2 us (0.934)
  the two profiles are of different devices: /device:TPU:24 before, /device:TPU:4 now
where the time goes in v1:
time: 96.2 us; the launch traced here: 96 us
  Pallas kernels  93.8 us (98%)
  local copies, waits for them, and re-layouts  2.26 us (2%)
    pallas_call x1, Pallas kernels, on_device(): pl.pallas_call(functools.partial(kernel, rows, cols, lags, split, width *...  93.8 us
    unnamed x1, local copies, waits for them, and re-layouts  2.26 us

profile of v1, /device:TPU:4, one launch (start us, length us, event | category | flops | bytes accessed | tf_op | source)
XLA Modules:
  0.0 96.0 jit_solution(160095839925347894)
XLA Ops:
  0.0 93.8 %shard_map.28 = bf16[512,1024]{1,0:T(8,128)(2,1)} custom-call(bf16[2,128,2048]{2,1,0:T(8,128)(2,1)} %bitcast.1, s32[4,4]{1,0:T(4,128)} %live_ref.1), custom_call_target="tpu_custom_call" | custom-call | tf_op jit(solution)/shard_map/pallas_call | solution.py:323
  93.8 2.3 %copy.4 = bf16[512,1024]{1,0:T(8,128)(2,1)} copy(bf16[512,1024]{1,0:T(8,128)(2,1)} %shard_map.28) | data formatting | bytes 2097152

commit v2 on v1

v2 whole, which is shorter than its diff:
```python
import functools

import jax
import jax.numpy as jnp
from jax import lax
from jax.experimental import pallas as pl
from jax.experimental.pallas import tpu as pltpu
from jax.sharding import PartitionSpec as P

MESH = pl.DeviceIdType.MESH
SPLIT = 2
SUB = 2
BEHIND = 2
NT_DIMS = (((1,), (1,)), ((), ()))


def kernel(
    rows, cols, lags, split, samples,
    x_ref, live_ref, out_ref,
    rb, rn, cn, tile, got, turned, done,
    own_sem, z_send, z_recv, c_send, c_recv, t_send, t_recv, m_send, m_recv,
):
    r, c, l = lax.axis_index("row"), lax.axis_index("col"), lax.axis_index("lag")
    units = cols * split
    m = rb.shape[1]
    mine = units // lags
    bits = rows.bit_length() - 1
    node = lax.bitwise_xor(r, c)
    base = jnp.where(node == 0, 0, units)
    chunk = m // SUB

    at_end = jnp.logical_or(c == 0, c == cols - 1)
    inside = jnp.logical_and(r > 0, r < rows - 1)
    lo = jnp.where(inside, 1, 0)
    hi = jnp.where(inside, cols - 2, cols - 1)
    computes = jnp.logical_not(jnp.logical_and(inside, at_end))
    mirrors = jnp.logical_not(jnp.logical_or(inside, at_end))
    paired = jnp.logical_or(mirrors, jnp.logical_not(computes))

    def place(u, where):
        k = u // split
        e = u - k * split
        left, right = where, cols - 1 - where
        d = jnp.abs(k - where)
        both = jnp.logical_and(d <= left, d <= right)
        before = split * (1 + jnp.minimum(d - 1, left) + jnp.minimum(d - 1, right))
        far = before + jnp.where(both, 2 * e + jnp.where(k > where, 1, 0), e)
        return jnp.where(d == 0, e, far)

    def unit_of(p):
        left, right = c, cols - 1 - c
        near = jnp.minimum(left, right)
        p1 = jnp.maximum(p - split, 0)
        p2 = jnp.maximum(p1 - 2 * split * near, 0)
        close = p1 < 2 * split * near
        d1 = p1 // (2 * split)
        rest = p1 - d1 * (2 * split)
        e1 = rest // 2
        s1 = rest - 2 * e1
        d2 = p2 // split
        e2 = p2 - d2 * split
        s2 = jnp.where(left < right, 1, 0)
        d = jnp.where(close, d1 + 1, d2 + near + 1)
        e = jnp.where(close, e1, e2)
        s = jnp.where(close, s1, s2)
        k = jnp.where(s == 0, c - d, c + d)
        k = jnp.clip(k, 0, cols - 1)
        return jnp.where(p < split, c * split + p, k * split + e)

    def along(side, u, p, h, src=None):
        to = jnp.clip(c + 1 - 2 * side, 0, cols - 1)
        rows_of = pl.ds(h * chunk, chunk)
        return pltpu.make_async_remote_copy(
            rb.at[p, rows_of] if src is None else src.at[p, rows_of],
            rb.at[place(u, to), rows_of],
            z_send.at[side, u, h], z_recv.at[u, h],
            device_id={"col": to}, device_id_type=MESH,
        )

    def down(bit, p, h):
        rows_of = pl.ds(h * chunk, chunk)
        return pltpu.make_async_remote_copy(
            rb.at[base + p, rows_of], rb.at[units + p, rows_of],
            c_send.at[bit, p, h], c_recv.at[p, h],
            device_id={"row": lax.bitwise_xor(r, 1 << bit)}, device_id_type=MESH,
        )

    def has_child(bit):
        return lax.rem(node, 2 << bit) == 0

    def across(i, j):
        owner = i // mine
        hop = lax.rem(owner - l + lags, lags)
        slot = jnp.maximum(hop - 1, 0)
        return pltpu.make_async_remote_copy(
            tile.at[i, j], got.at[slot, lax.rem(i, mine), j],
            t_send.at[i, j], t_recv.at[slot, lax.rem(i, mine), j],
            device_id={"lag": owner}, device_id_type=MESH,
        )

    def mirror(kk, j):
        i = l * mine + kk
        return pltpu.make_async_remote_copy(
            turned.at[kk, j], done.at[lax.rem(j, mine), i],
            m_send.at[kk, j], m_recv.at[lax.rem(j, mine), i],
            device_id={"row": c, "col": r, "lag": j // mine}, device_id_type=MESH,
        )

    own = pltpu.make_async_copy(x_ref, rb.at[pl.ds(0, split)], own_sem)
    own.start()

    barrier = pltpu.get_barrier_semaphore()
    for j in range(1, rows):
        pl.semaphore_signal(
            barrier, device_id={"row": lax.rem(r + j, rows)}, device_id_type=MESH
        )
    for j in range(1, lags):
        pl.semaphore_signal(
            barrier, device_id={"lag": lax.rem(l + j, lags)}, device_id_type=MESH
        )

    @pl.when(c > 0)
    def _():
        pl.semaphore_signal(barrier, device_id={"col": c - 1}, device_id_type=MESH)

    @pl.when(c < cols - 1)
    def _():
        pl.semaphore_signal(barrier, device_id={"col": c + 1}, device_id_type=MESH)

    @pl.when(paired)
    def _():
        for o in range(lags):
            pl.semaphore_signal(
                barrier, device_id={"row": c, "col": r, "lag": o}, device_id_type=MESH
            )

    beside = jnp.where(at_end, 1, 2) + jnp.where(paired, lags, 0)
    pl.semaphore_wait(barrier, rows - 1 + lags - 1 + beside)

    def goes_on(side):
        return c < hi if side == 0 else c > lo

    for side in range(2):

        @pl.when(goes_on(side))
        def _():
            for e in range(split):
                for h in range(SUB):
                    along(side, c * split + e, e, h, x_ref).start()

    own.wait()
    live = live_ref[r, c].astype(jnp.float32)

    def keep(i, j, distance):
        tile[i, j] = distance

        @pl.when(i // mine != l)
        def _():
            across(i, j).start()

    def strips(n, un):
        def inner_of(a, b):
            return lax.dot_general(a, b, NT_DIMS, preferred_element_type=jnp.float32)

        def two(at):
            return rb[pl.ds(at, 2)].reshape(2 * m, rb.shape[2])

        def row_pair(t, carry):
            inner = inner_of(rb[n], two(base + 2 * t))
            for o in range(2):
                j = 2 * t + o
                keep(
                    un, unit_of(j),
                    rn[n][:, :1] + cn[j][:1] - 2.0 * inner[:, o * m : (o + 1) * m],
                )
            return carry

        def column_pair(t, carry):
            inner = inner_of(two(2 * t), rb[base + n])
            for o in range(2):
                i = 2 * t + o
                keep(
                    unit_of(i), un,
                    rn[i][:, :1] + cn[n][:1] - 2.0 * inner[o * m : (o + 1) * m],
                )
            return carry

        def single(i, j):
            inner = inner_of(rb[i], rb[base + j])
            keep(unit_of(i), unit_of(j), rn[i][:, :1] + cn[j][:1] - 2.0 * inner)

        odd = lax.rem(n, 2)
        lax.fori_loop(0, (n + 1) // 2, row_pair, 0)

        def last_one(t, carry):
            single(n - odd, n)
            return carry

        lax.fori_loop(0, 1, last_one, 0)
        lax.fori_loop(0, n // 2, column_pair, 0)

    def finish(n, un):
        def close(i, j):
            kk = lax.rem(i, mine)
            total = tile[i, j]
            for o in range(lags - 1):
                pltpu.make_async_remote_copy(
                    tile.at[i, j], got.at[o, kk, j], t_send.at[i, j],
                    t_recv.at[o, kk, j],
                    device_id={"lag": lax.rem(l + 1, lags)},
                    device_id_type=MESH,
                ).wait_recv()
                total = total + got[o, kk, j]
            gram = jnp.exp(-2.0 * total / samples) * live
            done[kk, j] = gram.astype(done.dtype)

            @pl.when(mirrors)
            def _():
                turned[kk, j] = gram.T.astype(turned.dtype)
                mirror(kk, j).start()

        def one(t, carry):
            ut = unit_of(jnp.minimum(t, 2 * n - t))
            i = jnp.where(t <= n, un, ut)
            j = jnp.where(t <= n, ut, un)

            @pl.when(i // mine == l)
            def _():
                close(i, j)

            return carry

        lax.fori_loop(0, 2 * n + 1, one, 0)

    def step(n, carry):
        u = unit_of(n)
        k = u // split

        @pl.when(jnp.logical_and(n >= split, computes))
        def _():
            for h in range(SUB):
                along(0, u, n, h).wait_recv()
                for side in range(2):
                    onward = k < c if side == 0 else k > c

                    @pl.when(jnp.logical_and(onward, goes_on(side)))
                    def _():
                        along(side, u, n, h).start()

                @pl.when(node == 0)
                def _():
                    for bit in reversed(range(bits)):
                        down(bit, n, h).start()

        @pl.when(jnp.logical_and(n < split, node == 0))
        def _():
            for h in range(SUB):
                for bit in reversed(range(bits)):
                    down(bit, n, h).start()

        @pl.when(node != 0)
        def _():
            for h in range(SUB):
                down(0, n, h).wait_recv()
                for bit in reversed(range(bits)):

                    @pl.when(has_child(bit))
                    def _():
                        down(bit, n, h).start()

        @pl.when(computes)
        def _():
            a = rb[n].astype(jnp.float32)
            rn[n] = jnp.broadcast_to(
                jnp.sum(a * a, axis=1, keepdims=True), rn.shape[1:]
            )
            b = rb[base + n].astype(jnp.float32)
            s = jnp.broadcast_to(jnp.sum(b * b, axis=1, keepdims=True), (m, 128))
            cn[n] = s.T[:8]
            strips(n, u)

            @pl.when(n >= BEHIND)
            def _():
                finish(n - BEHIND, unit_of(n - BEHIND))

        return carry

    lax.fori_loop(0, units, step, 0)

    @pl.when(computes)
    def _():
        def tail(n, carry):
            finish(n, unit_of(n))
            return carry

        lax.fori_loop(units - BEHIND, units, tail, 0)

    @pl.when(jnp.logical_not(computes))
    def _():
        def landed(t, carry):
            kk, i = t // units, lax.rem(t, units)
            pltpu.make_async_remote_copy(
                turned.at[0, 0], done.at[kk, i], m_send.at[0, 0], m_recv.at[kk, i],
                device_id={"row": c, "col": r, "lag": i // mine}, device_id_type=MESH,
            ).wait_recv()
            return carry

        lax.fori_loop(0, mine * units, landed, 0)

    def lay(kk, carry):
        for j in range(units):
            out_ref[pl.ds(kk * m, m), j * m : (j + 1) * m] = done[kk, j]
        return carry

    lax.fori_loop(0, mine, lay, 0)

    def drain(p, carry):
        u = unit_of(p)
        k = u // split
        got_it = jnp.logical_or(k == c, computes)
        for h in range(SUB):

            @pl.when(jnp.logical_and(got_it, jnp.logical_and(k <= c, goes_on(0))))
            def _():
                along(0, u, p, h).wait_send()

            @pl.when(jnp.logical_and(got_it, jnp.logical_and(k >= c, goes_on(1))))
            def _():
                along(1, u, p, h).wait_send()

            for bit in range(bits):

                @pl.when(has_child(bit))
                def _():
                    down(bit, p, h).wait_send()

        @pl.when(jnp.logical_and(u // mine != l, computes))
        def _():
            def each(j, carry):
                across(u, j).wait_send()
                return carry

            lax.fori_loop(0, units, each, 0)

        return carry

    lax.fori_loop(0, units, drain, 0)

    @pl.when(mirrors)
    def _():
        def sent(t, carry):
            mirror(t // units, lax.rem(t, units)).wait_send()
            return carry

        lax.fori_loop(0, mine * units, sent, 0)


def on_device(rows, cols, lags, trajectories, pair_live):
    held, width = trajectories.shape
    split = SPLIT if held % (SPLIT * 128) == 0 else 1
    m = held // split
    units = cols * split
    mine = units // lags
    bits = rows.bit_length() - 1
    dma = pltpu.SemaphoreType.DMA
    return pl.pallas_call(
        functools.partial(kernel, rows, cols, lags, split, width * lags),
        out_shape=jax.ShapeDtypeStruct((mine * m, units * m), jnp.bfloat16),
        in_specs=[
            pl.BlockSpec(memory_space=pl.ANY),
            pl.BlockSpec(memory_space=pltpu.SMEM),
        ],
        out_specs=pl.BlockSpec(memory_space=pltpu.VMEM),
        scratch_shapes=[
            pltpu.VMEM((2 * units, m, width), jnp.bfloat16),
            pltpu.VMEM((units, m, 128), jnp.float32),
            pltpu.VMEM((units, 8, m), jnp.float32),
            pltpu.VMEM((units, units, m, m), jnp.float32),
            pltpu.VMEM((lags - 1, mine, units, m, m), jnp.float32),
            pltpu.VMEM((mine, units, m, m), jnp.bfloat16),
            pltpu.VMEM((mine, units, m, m), jnp.bfloat16),
            dma,
            dma((2, units, SUB)),
            dma((units, SUB)),
            dma((bits, units, SUB)),
            dma((units, SUB)),
            dma((units, units)),
            dma((lags - 1, mine, units)),
            dma((mine, units)),
            dma((mine, units)),
        ],
        compiler_params=pltpu.CompilerParams(
            collective_id=0, has_side_effects=True, vmem_limit_bytes=60 * 2**20
        ),
    )(trajectories.reshape(split, m, width), pair_live)


def solution(mesh):
    size = mesh.shape
    return jax.shard_map(
        functools.partial(on_device, size["row"], size["col"], size["lag"]),
        mesh=mesh,
        in_specs=(P(("row", "col"), "lag"), P()),
        out_specs=P(("row", "lag"), "col"),
        check_vma=False,
    )
```

time: 96.2 us -> 87.3 us (0.907)
  Pallas kernels: 93.8 us -> 84.9 us
    pallas_call x1, Pallas kernels: 93.8 us -> 84.9 us  [on_device(): pl.pallas_call(functools.partial(kernel, rows, cols, lags, split, width *...]
where the time goes in v2:
time: 87.3 us; the launch traced here: 87.1 us
  Pallas kernels  84.9 us (97%)
  local copies, waits for them, and re-layouts  2.26 us (3%)
    pallas_call x1, Pallas kernels, on_device(): pl.pallas_call(functools.partial(kernel, rows, cols, lags, split, width *...  84.9 us
    unnamed x1, local copies, waits for them, and re-layouts  2.26 us

profile of v2, /device:TPU:4, one launch (start us, length us, event | category | flops | bytes accessed | tf_op | source)
XLA Modules:
  0.0 87.1 jit_solution(9073632500528133463)
XLA Ops:
  0.0 84.9 %shard_map.28 = bf16[512,1024]{1,0:T(8,128)(2,1)} custom-call(bf16[2,128,2048]{2,1,0:T(8,128)(2,1)} %bitcast.1, s32[4,4]{1,0:T(4,128)} %live_ref.1), custom_call_target="tpu_custom_call" | custom-call | tf_op jit(solution)/shard_map/pallas_call | solution.py:366
  84.9 2.3 %copy.4 = bf16[512,1024]{1,0:T(8,128)(2,1)} copy(bf16[512,1024]{1,0:T(8,128)(2,1)} %shard_map.28) | data formatting | bytes 2097152

commit v3 on v2

--- a/solution.py
+++ b/solution.py
@@ -10,7 +10,7 @@
 MESH = pl.DeviceIdType.MESH
 SPLIT = 2
 SUB = 2
-BEHIND = 2
+BEHIND = 3
 NT_DIMS = (((1,), (1,)), ((), ()))
 
 
@@ -38,13 +38,14 @@
     paired = jnp.logical_or(mirrors, jnp.logical_not(computes))
 
     def place(u, where):
-        k = u // split
+        k = lax.div(u, split)
         e = u - k * split
         left, right = where, cols - 1 - where
         d = jnp.abs(k - where)
         both = jnp.logical_and(d <= left, d <= right)
         before = split * (1 + jnp.minimum(d - 1, left) + jnp.minimum(d - 1, right))
-        far = before + jnp.where(both, 2 * e + jnp.where(k > where, 1, 0), e)
+        second = (k > where) != (left < right)
+        far = before + jnp.where(both, 2 * e + jnp.where(second, 1, 0), e)
         return jnp.where(d == 0, e, far)
 
     def unit_of(p):
@@ -56,7 +57,7 @@
         d1 = p1 // (2 * split)
         rest = p1 - d1 * (2 * split)
         e1 = rest // 2
-        s1 = rest - 2 * e1
+        s1 = jnp.where(left < right, 1 - rest + 2 * e1, rest - 2 * e1)
         d2 = p2 // split
         e2 = p2 - d2 * split
         s2 = jnp.where(left < right, 1, 0)
@@ -89,7 +90,7 @@
         return lax.rem(node, 2 << bit) == 0
 
     def across(i, j):
-        owner = i // mine
+        owner = lax.div(i, mine)
         hop = lax.rem(owner - l + lags, lags)
         slot = jnp.maximum(hop - 1, 0)
         return pltpu.make_async_remote_copy(
@@ -103,8 +104,16 @@
         return pltpu.make_async_remote_copy(
             turned.at[kk, j], done.at[lax.rem(j, mine), i],
             m_send.at[kk, j], m_recv.at[lax.rem(j, mine), i],
-            device_id={"row": c, "col": r, "lag": j // mine}, device_id_type=MESH,
-        )
+            device_id={"row": c, "col": r, "lag": lax.div(j, mine)}, device_id_type=MESH,
+        )
+
+    at = [unit_of(jnp.int32(p)) for p in range(units)]
+
+    def order(p):
+        u = at[-1]
+        for i in range(units - 1):
+            u = jnp.where(p == i, at[i], u)
+        return u
 
     own = pltpu.make_async_copy(x_ref, rb.at[pl.ds(0, split)], own_sem)
     own.start()
@@ -151,94 +160,97 @@
     own.wait()
     live = live_ref[r, c].astype(jnp.float32)
 
-    def keep(i, j, distance):
-        tile[i, j] = distance
-
-        @pl.when(i // mine != l)
+    def inner_of(a, b):
+        return lax.dot_general(a, b, NT_DIMS, preferred_element_type=jnp.float32)
+
+    def two(at):
+        return rb[pl.ds(at, 2)].reshape(2 * m, rb.shape[2])
+
+    def keep(p, q, inner, held=False):
+        i, j = order(p), order(q)
+        tile[i, j] = rn[p][:, :1] + cn[q][:1] - 2.0 * inner
+
+        @pl.when(jnp.logical_and(lax.div(i, mine) != l, jnp.logical_not(held)))
         def _():
             across(i, j).start()
 
-    def strips(n, un):
-        def inner_of(a, b):
-            return lax.dot_general(a, b, NT_DIMS, preferred_element_type=jnp.float32)
-
-        def two(at):
-            return rb[pl.ds(at, 2)].reshape(2 * m, rb.shape[2])
-
-        def row_pair(t, carry):
-            inner = inner_of(rb[n], two(base + 2 * t))
-            for o in range(2):
-                j = 2 * t + o
-                keep(
-                    un, unit_of(j),
-                    rn[n][:, :1] + cn[j][:1] - 2.0 * inner[:, o * m : (o + 1) * m],
-                )
+    def holds(n):
+        return jnp.logical_and(n == units - 2, inside)
+
+    def release(n):
+        i = order(n)
+
+        @pl.when(lax.div(i, mine) != l)
+        def _():
+            loop(n, lambda q: across(i, order(q)).start())
+
+    def wide(n, t):
+        inner = inner_of(rb[n], two(base + 2 * t))
+        for j in range(2):
+            keep(n, 2 * t + j, inner[:, j * m : (j + 1) * m], holds(n))
+
+    def tall(s, n):
+        inner = inner_of(two(2 * s), rb[base + n])
+        for i in range(2):
+            keep(2 * s + i, n, inner[i * m : (i + 1) * m])
+
+    def loop(count, body):
+        def one(t, carry):
+            body(t)
             return carry
 
-        def column_pair(t, carry):
-            inner = inner_of(two(2 * t), rb[base + n])
-            for o in range(2):
-                i = 2 * t + o
-                keep(
-                    unit_of(i), un,
-                    rn[i][:, :1] + cn[n][:1] - 2.0 * inner[o * m : (o + 1) * m],
-                )
-            return carry
-
-        def single(i, j):
-            inner = inner_of(rb[i], rb[base + j])
-            keep(unit_of(i), unit_of(j), rn[i][:, :1] + cn[j][:1] - 2.0 * inner)
-
-        odd = lax.rem(n, 2)
-        lax.fori_loop(0, (n + 1) // 2, row_pair, 0)
-
-        def last_one(t, carry):
-            single(n - odd, n)
-            return carry
-
-        lax.fori_loop(0, 1, last_one, 0)
-        lax.fori_loop(0, n // 2, column_pair, 0)
-
-    def finish(n, un):
-        def close(i, j):
-            kk = lax.rem(i, mine)
-            total = tile[i, j]
-            for o in range(lags - 1):
-                pltpu.make_async_remote_copy(
-                    tile.at[i, j], got.at[o, kk, j], t_send.at[i, j],
-                    t_recv.at[o, kk, j],
-                    device_id={"lag": lax.rem(l + 1, lags)},
-                    device_id_type=MESH,
-                ).wait_recv()
-                total = total + got[o, kk, j]
-            gram = jnp.exp(-2.0 * total / samples) * live
-            done[kk, j] = gram.astype(done.dtype)
-
-            @pl.when(mirrors)
-            def _():
-                turned[kk, j] = gram.T.astype(turned.dtype)
+        lax.fori_loop(0, count, one, 0)
+
+    def close(p, q, sends):
+        i, j = order(p), order(q)
+        kk = lax.rem(i, mine)
+        total = tile[i, j]
+        for o in range(lags - 1):
+            pltpu.make_async_remote_copy(
+                tile.at[i, j], got.at[o, kk, j], t_send.at[i, j], t_recv.at[o, kk, j],
+                device_id={"lag": lax.rem(l + 1, lags)}, device_id_type=MESH,
+            ).wait_recv()
+            total = total + got[o, kk, j]
+        gram = jnp.exp(-2.0 * total / samples) * live
+        done[kk, j] = gram.astype(done.dtype)
+
+        @pl.when(mirrors)
+        def _():
+            turned[kk, j] = gram.T.astype(turned.dtype)
+
+            @pl.when(sends)
+            def _():
                 mirror(kk, j).start()
 
-        def one(t, carry):
-            ut = unit_of(jnp.minimum(t, 2 * n - t))
-            i = jnp.where(t <= n, un, ut)
-            j = jnp.where(t <= n, ut, un)
-
-            @pl.when(i // mine == l)
-            def _():
-                close(i, j)
-
-            return carry
-
-        lax.fori_loop(0, 2 * n + 1, one, 0)
-
-    def step(n, carry):
-        u = unit_of(n)
-        k = u // split
-
-        @pl.when(jnp.logical_and(n >= split, computes))
-        def _():
-            for h in range(SUB):
+    def finish(n, sends):
+        def one(p, q):
+            @pl.when(lax.div(order(p), mine) == l)
+            def _():
+                close(p, q, sends)
+
+        @pl.when(lax.div(order(n), mine) == l)
+        def _():
+            loop(n + 1, lambda q: close(n, q, sends))
+
+        loop(n, lambda p: one(p, n))
+
+    early = units - 2 - BEHIND
+    near = jnp.abs(c - r) < 2
+
+    def send_mirrored(p):
+        i = order(p)
+
+        @pl.when(lax.div(i, mine) == l)
+        def _():
+            loop(early, lambda q: mirror(lax.rem(i, mine), order(q)).start())
+
+    def gather_rows(n):
+        u = order(n)
+        k = lax.div(u, split)
+        for h in range(SUB):
+
+            @pl.when(jnp.logical_and(n >= split, computes))
+            def _():
                 along(0, u, n, h).wait_recv()
                 for side in range(2):
                     onward = k < c if side == 0 else k > c
@@ -247,17 +259,12 @@
                     def _():
                         along(side, u, n, h).start()
 
-                @pl.when(node == 0)
-                def _():
-                    for bit in reversed(range(bits)):
-                        down(bit, n, h).start()
-
-        @pl.when(jnp.logical_and(n < split, node == 0))
-        def _():
-            for h in range(SUB):
+            @pl.when(node == 0)
+            def _():
                 for bit in reversed(range(bits)):
                     down(bit, n, h).start()
 
+    def gather_columns(n):
         @pl.when(node != 0)
         def _():
             for h in range(SUB):
@@ -268,32 +275,56 @@
                     def _():
                         down(bit, n, h).start()
 
+    def row_norms(n):
+        a = rb[n].astype(jnp.float32)
+        rn[n] = jnp.broadcast_to(jnp.sum(a * a, axis=1, keepdims=True), rn.shape[1:])
+
+    def column_norms(n):
+        b = rb[base + n].astype(jnp.float32)
+        s = jnp.broadcast_to(jnp.sum(b * b, axis=1, keepdims=True), (m, 128))
+        cn[n] = s.T[:8]
+
+    def step(n):
+        odd = lax.rem(n, 2)
+        gather_rows(n)
+
         @pl.when(computes)
         def _():
-            a = rb[n].astype(jnp.float32)
-            rn[n] = jnp.broadcast_to(
-                jnp.sum(a * a, axis=1, keepdims=True), rn.shape[1:]
-            )
-            b = rb[base + n].astype(jnp.float32)
-            s = jnp.broadcast_to(jnp.sum(b * b, axis=1, keepdims=True), (m, 128))
-            cn[n] = s.T[:8]
-            strips(n, u)
+            row_norms(n)
+            loop(lax.div(n, 2), lambda t: wide(n, t))
+
+            @pl.when(odd == 1)
+            def _():
+                keep(n, n - 1, inner_of(rb[n], rb[base + n - 1]), holds(n))
+
+            @pl.when(holds(n - 1))
+            def _():
+                release(n - 1)
+
+        gather_columns(n)
+
+        @pl.when(computes)
+        def _():
+            column_norms(n)
+            loop(lax.div(n + 1, 2), lambda t: tall(t, n))
+
+            @pl.when(odd == 0)
+            def _():
+                keep(n, n, inner_of(rb[n], rb[base + n]))
 
             @pl.when(n >= BEHIND)
             def _():
-                finish(n - BEHIND, unit_of(n - BEHIND))
-
-        return carry
-
-    lax.fori_loop(0, units, step, 0)
+                @pl.when(jnp.logical_and(n == units - 2, jnp.logical_and(mirrors, jnp.logical_not(near))))
+                def _():
+                    loop(early, send_mirrored)
+
+                finish(n - BEHIND, jnp.logical_or(near, n >= units - 2))
+
+    loop(units, step)
 
     @pl.when(computes)
     def _():
-        def tail(n, carry):
-            finish(n, unit_of(n))
-            return carry
-
-        lax.fori_loop(units - BEHIND, units, tail, 0)
+        loop(BEHIND, lambda o: finish(units - BEHIND + o, True))
 
     @pl.when(jnp.logical_not(computes))
     def _():
@@ -315,8 +346,8 @@
     lax.fori_loop(0, mine, lay, 0)
 
     def drain(p, carry):
-        u = unit_of(p)
-        k = u // split
+        u = order(p)
+        k = lax.div(u, split)
         got_it = jnp.logical_or(k == c, computes)
         for h in range(SUB):
 
@@ -334,7 +365,7 @@
                 def _():
                     down(bit, p, h).wait_send()
 
-        @pl.when(jnp.logical_and(u // mine != l, computes))
+        @pl.when(jnp.logical_and(lax.div(u, mine) != l, computes))
         def _():
             def each(j, carry):
                 across(u, j).wait_send()

time: 87.3 us -> 83.8 us (0.960); the launches traced: 87.1 us -> 82.5 us
  Pallas kernels: 84.9 us -> 80.2 us
    pallas_call x1, Pallas kernels: 84.9 us -> 80.2 us  [on_device(): pl.pallas_call(functools.partial(kernel, rows, cols, lags, split, width *...]
where the time goes in v3:
time: 83.8 us; the launch traced here: 82.5 us
  Pallas kernels  80.2 us (96%)
  local copies, waits for them, and re-layouts  2.26 us (3%)
    pallas_call x1, Pallas kernels, on_device(): pl.pallas_call(functools.partial(kernel, rows, cols, lags, split, width *...  80.2 us
    unnamed x1, local copies, waits for them, and re-layouts  2.26 us

profile of v3, /device:TPU:4, one launch (start us, length us, event | category | flops | bytes accessed | tf_op | source)
XLA Modules:
  0.0 82.5 jit_solution(11371831460121032540)
XLA Ops:
  0.0 80.2 %shard_map.28 = bf16[512,1024]{1,0:T(8,128)(2,1)} custom-call(bf16[2,128,2048]{2,1,0:T(8,128)(2,1)} %bitcast.1, s32[4,4]{1,0:T(4,128)} %live_ref.1), custom_call_target="tpu_custom_call" | custom-call | tf_op jit(solution)/shard_map/pallas_call | solution.py:397
  80.2 2.3 %copy.4 = bf16[512,1024]{1,0:T(8,128)(2,1)} copy(bf16[512,1024]{1,0:T(8,128)(2,1)} %shard_map.28) | data formatting | bytes 2097152

commit v4 on v3

--- a/solution.py
+++ b/solution.py
@@ -10,14 +10,14 @@
 MESH = pl.DeviceIdType.MESH
 SPLIT = 2
 SUB = 2
-BEHIND = 3
+BEHIND = 2
 NT_DIMS = (((1,), (1,)), ((), ()))
 
 
 def kernel(
     rows, cols, lags, split, samples,
-    x_ref, live_ref, out_ref,
-    rb, rn, cn, tile, got, turned, done,
+    x_ref, live_ref, result,
+    out_ref, out_sem, rb, rn, cn, tile, got, turned, done,
     own_sem, z_send, z_recv, c_send, c_recv, t_send, t_recv, m_send, m_recv,
 ):
     r, c, l = lax.axis_index("row"), lax.axis_index("col"), lax.axis_index("lag")
@@ -31,11 +31,49 @@
 
     at_end = jnp.logical_or(c == 0, c == cols - 1)
     inside = jnp.logical_and(r > 0, r < rows - 1)
-    lo = jnp.where(inside, 1, 0)
-    hi = jnp.where(inside, cols - 2, cols - 1)
-    computes = jnp.logical_not(jnp.logical_and(inside, at_end))
+    partial = jnp.logical_and(inside, at_end)
+    limit = jnp.where(partial, mine, units)
     mirrors = jnp.logical_not(jnp.logical_or(inside, at_end))
-    paired = jnp.logical_or(mirrors, jnp.logical_not(computes))
+    on_diagonal = r == c
+    turns = jnp.logical_and(on_diagonal, jnp.logical_not(at_end))
+    swaps = jnp.logical_and(inside, jnp.logical_not(jnp.logical_or(at_end, on_diagonal)))
+    paired = jnp.logical_not(jnp.logical_or(on_diagonal, jnp.logical_and(at_end, jnp.logical_not(partial))))
+
+    first = jnp.where(on_diagonal, 2 * c < cols, c < r)
+    early = jnp.where(first, 0, lags - 1)
+    late = lags - 1 - early
+
+    def near_lag(end):
+        return jnp.where(end == 0, 0, lags - 1)
+
+    def gives(a, b):
+        given = jnp.logical_and(mirrors, b != near_lag(r))
+        if lags == 1:
+            return given
+        swap = jnp.logical_and(swaps, jnp.logical_and(a == early, b == early))
+        turn = jnp.logical_and(turns, jnp.logical_and(a == early, b != early))
+        return jnp.logical_or(given, jnp.logical_or(swap, turn))
+
+    def takes(a, b):
+        taken = jnp.logical_and(partial, a != near_lag(c))
+        if lags == 1:
+            return taken
+        swap = jnp.logical_and(swaps, jnp.logical_and(a == late, b == late))
+        turn = jnp.logical_and(turns, jnp.logical_and(a != early, b == early))
+        return jnp.logical_or(taken, jnp.logical_or(swap, turn))
+
+    def double(p, q, a, b):
+        return jnp.logical_and(on_diagonal, jnp.logical_and(a == b, p < q))
+
+    def sent(p, q):
+        a, b = lax.div(order(p), mine), lax.div(order(q), mine)
+        skipped = jnp.logical_or(takes(a, b), double(p, q, a, b))
+        return jnp.logical_and(a != l, jnp.logical_not(skipped))
+
+    def closed(p, q):
+        a, b = lax.div(order(p), mine), lax.div(order(q), mine)
+        skipped = jnp.logical_or(takes(a, b), double(p, q, a, b))
+        return jnp.logical_and(a == l, jnp.logical_not(skipped))
 
     def place(u, where):
         k = lax.div(u, split)
@@ -146,14 +184,17 @@
     beside = jnp.where(at_end, 1, 2) + jnp.where(paired, lags, 0)
     pl.semaphore_wait(barrier, rows - 1 + lags - 1 + beside)
 
-    def goes_on(side):
-        return c < hi if side == 0 else c > lo
+    def goes_on(side, u):
+        a = lax.div(u, mine)
+        if side == 0:
+            return c < jnp.where(jnp.logical_and(inside, a != lags - 1), cols - 2, cols - 1)
+        return c > jnp.where(jnp.logical_and(inside, a != 0), 1, 0)
 
     for side in range(2):
-
-        @pl.when(goes_on(side))
-        def _():
-            for e in range(split):
+        for e in range(split):
+
+            @pl.when(goes_on(side, c * split + e))
+            def _():
                 for h in range(SUB):
                     along(side, c * split + e, e, h, x_ref).start()
 
@@ -170,7 +211,7 @@
         i, j = order(p), order(q)
         tile[i, j] = rn[p][:, :1] + cn[q][:1] - 2.0 * inner
 
-        @pl.when(jnp.logical_and(lax.div(i, mine) != l, jnp.logical_not(held)))
+        @pl.when(jnp.logical_and(sent(p, q), jnp.logical_not(held)))
         def _():
             across(i, j).start()
 
@@ -180,9 +221,12 @@
     def release(n):
         i = order(n)
 
-        @pl.when(lax.div(i, mine) != l)
-        def _():
-            loop(n, lambda q: across(i, order(q)).start())
+        def one(q):
+            @pl.when(sent(n, q))
+            def _():
+                across(i, order(q)).start()
+
+        loop(n, one)
 
     def wide(n, t):
         inner = inner_of(rb[n], two(base + 2 * t))
@@ -214,7 +258,11 @@
         gram = jnp.exp(-2.0 * total / samples) * live
         done[kk, j] = gram.astype(done.dtype)
 
-        @pl.when(mirrors)
+        @pl.when(double(q, p, lax.div(i, mine), lax.div(j, mine)))
+        def _():
+            done[lax.rem(j, mine), i] = gram.T.astype(done.dtype)
+
+        @pl.when(gives(l, lax.div(j, mine)))
         def _():
             turned[kk, j] = gram.T.astype(turned.dtype)
 
@@ -224,38 +272,40 @@
 
     def finish(n, sends):
         def one(p, q):
-            @pl.when(lax.div(order(p), mine) == l)
+            @pl.when(closed(p, q))
             def _():
                 close(p, q, sends)
 
-        @pl.when(lax.div(order(n), mine) == l)
-        def _():
-            loop(n + 1, lambda q: close(n, q, sends))
-
+        loop(n + 1, lambda q: one(n, q))
         loop(n, lambda p: one(p, n))
 
-    early = units - 2 - BEHIND
-    near = jnp.abs(c - r) < 2
+    soon = units - BEHIND
+    prompt = jnp.logical_or(on_diagonal, jnp.logical_and(mirrors, jnp.abs(c - r) < 2))
 
     def send_mirrored(p):
         i = order(p)
 
-        @pl.when(lax.div(i, mine) == l)
-        def _():
-            loop(early, lambda q: mirror(lax.rem(i, mine), order(q)).start())
+        def one(q):
+            j = order(q)
+
+            @pl.when(jnp.logical_and(closed(p, q), gives(l, lax.div(j, mine))))
+            def _():
+                mirror(lax.rem(i, mine), j).start()
+
+        loop(soon, one)
 
     def gather_rows(n):
         u = order(n)
         k = lax.div(u, split)
         for h in range(SUB):
 
-            @pl.when(jnp.logical_and(n >= split, computes))
+            @pl.when(jnp.logical_and(n >= split, n < limit))
             def _():
                 along(0, u, n, h).wait_recv()
                 for side in range(2):
                     onward = k < c if side == 0 else k > c
 
-                    @pl.when(jnp.logical_and(onward, goes_on(side)))
+                    @pl.when(jnp.logical_and(onward, goes_on(side, u)))
                     def _():
                         along(side, u, n, h).start()
 
@@ -285,58 +335,56 @@
         cn[n] = s.T[:8]
 
     def step(n):
-        odd = lax.rem(n, 2)
         gather_rows(n)
 
-        @pl.when(computes)
+        @pl.when(n < limit)
         def _():
             row_norms(n)
             loop(lax.div(n, 2), lambda t: wide(n, t))
 
-            @pl.when(odd == 1)
+            @pl.when(lax.rem(n, 2) == 1)
             def _():
                 keep(n, n - 1, inner_of(rb[n], rb[base + n - 1]), holds(n))
 
-            @pl.when(holds(n - 1))
-            def _():
-                release(n - 1)
+        @pl.when(holds(n - 1))
+        def _():
+            release(n - 1)
 
         gather_columns(n)
-
-        @pl.when(computes)
-        def _():
-            column_norms(n)
-            loop(lax.div(n + 1, 2), lambda t: tall(t, n))
-
-            @pl.when(odd == 0)
-            def _():
-                keep(n, n, inner_of(rb[n], rb[base + n]))
-
-            @pl.when(n >= BEHIND)
-            def _():
-                @pl.when(jnp.logical_and(n == units - 2, jnp.logical_and(mirrors, jnp.logical_not(near))))
-                def _():
-                    loop(early, send_mirrored)
-
-                finish(n - BEHIND, jnp.logical_or(near, n >= units - 2))
+        column_norms(n)
+        count = jnp.minimum(n + 1, limit)
+        loop(lax.div(count, 2), lambda t: tall(t, n))
+
+        @pl.when(lax.rem(count, 2) == 1)
+        def _():
+            keep(count - 1, n, inner_of(rb[count - 1], rb[base + n]))
+
+        @pl.when(n >= BEHIND)
+        def _():
+            finish(n - BEHIND, prompt)
 
     loop(units, step)
 
-    @pl.when(computes)
+    @pl.when(jnp.logical_not(prompt))
     def _():
-        loop(BEHIND, lambda o: finish(units - BEHIND + o, True))
-
-    @pl.when(jnp.logical_not(computes))
-    def _():
-        def landed(t, carry):
-            kk, i = t // units, lax.rem(t, units)
+        loop(soon, send_mirrored)
+
+    loop(BEHIND, lambda o: finish(units - BEHIND + o, True))
+
+    def landed(t, carry):
+        kk, i = lax.div(t, units), lax.rem(t, units)
+
+        @pl.when(takes(l, lax.div(i, mine)))
+        def _():
             pltpu.make_async_remote_copy(
                 turned.at[0, 0], done.at[kk, i], m_send.at[0, 0], m_recv.at[kk, i],
-                device_id={"row": c, "col": r, "lag": i // mine}, device_id_type=MESH,
+                device_id={"row": c, "col": r, "lag": lax.div(i, mine)},
+                device_id_type=MESH,
             ).wait_recv()
-            return carry
-
-        lax.fori_loop(0, mine * units, landed, 0)
+
+        return carry
+
+    lax.fori_loop(0, mine * units, landed, 0)
 
     def lay(kk, carry):
         for j in range(units):
@@ -344,18 +392,20 @@
         return carry
 
     lax.fori_loop(0, mine, lay, 0)
+    put = pltpu.make_async_copy(out_ref, result, out_sem)
+    put.start()
 
     def drain(p, carry):
         u = order(p)
         k = lax.div(u, split)
-        got_it = jnp.logical_or(k == c, computes)
+        got_it = jnp.logical_or(k == c, p < limit)
         for h in range(SUB):
 
-            @pl.when(jnp.logical_and(got_it, jnp.logical_and(k <= c, goes_on(0))))
+            @pl.when(jnp.logical_and(got_it, jnp.logical_and(k <= c, goes_on(0, u))))
             def _():
                 along(0, u, p, h).wait_send()
 
-            @pl.when(jnp.logical_and(got_it, jnp.logical_and(k >= c, goes_on(1))))
+            @pl.when(jnp.logical_and(got_it, jnp.logical_and(k >= c, goes_on(1, u))))
             def _():
                 along(1, u, p, h).wait_send()
 
@@ -365,25 +415,30 @@
                 def _():
                     down(bit, p, h).wait_send()
 
-        @pl.when(jnp.logical_and(lax.div(u, mine) != l, computes))
-        def _():
-            def each(j, carry):
-                across(u, j).wait_send()
-                return carry
-
-            lax.fori_loop(0, units, each, 0)
+        def each(q, carry):
+            @pl.when(sent(p, q))
+            def _():
+                across(u, order(q)).wait_send()
+
+            return carry
+
+        lax.fori_loop(0, units, each, 0)
 
         return carry
 
     lax.fori_loop(0, units, drain, 0)
 
-    @pl.when(mirrors)
-    def _():
-        def sent(t, carry):
-            mirror(t // units, lax.rem(t, units)).wait_send()
-            return carry
-
-        lax.fori_loop(0, mine * units, sent, 0)
+    def gone(t, carry):
+        kk, j = lax.div(t, units), lax.rem(t, units)
+
+        @pl.when(gives(l, lax.div(j, mine)))
+        def _():
+            mirror(kk, j).wait_send()
+
+        return carry
+
+    lax.fori_loop(0, mine * units, gone, 0)
+    put.wait()
 
 
 def on_device(rows, cols, lags, trajectories, pair_live):
@@ -401,8 +456,10 @@
             pl.BlockSpec(memory_space=pl.ANY),
             pl.BlockSpec(memory_space=pltpu.SMEM),
         ],
-        out_specs=pl.BlockSpec(memory_space=pltpu.VMEM),
+        out_specs=pl.BlockSpec(memory_space=pl.ANY),
         scratch_shapes=[
+            pltpu.VMEM((mine * m, units * m), jnp.bfloat16),
+            dma,
             pltpu.VMEM((2 * units, m, width), jnp.bfloat16),
             pltpu.VMEM((units, m, 128), jnp.float32),
             pltpu.VMEM((units, 8, m), jnp.float32),

time: 83.8 us -> 82.1 us (0.980)
  the two profiles are of different devices: /device:TPU:4 before, /device:TPU:3 now
where the time goes in v4:
time: 82.1 us; the launch traced here: 81.9 us
  Pallas kernels  79.6 us (97%)
  local copies, waits for them, and re-layouts  2.26 us (3%)
    pallas_call x1, Pallas kernels, on_device(): pl.pallas_call(functools.partial(kernel, rows, cols, lags, split, width *...  79.6 us
    unnamed x1, local copies, waits for them, and re-layouts  2.26 us

profile of v4, /device:TPU:3, one launch (start us, length us, event | category | flops | bytes accessed | tf_op | source)
XLA Modules:
  0.0 81.9 jit_solution(16488723562158743805)
XLA Ops:
  0.0 79.6 %shard_map.28 = bf16[512,1024]{1,0:T(8,128)(2,1)} custom-call(bf16[2,128,2048]{2,1,0:T(8,128)(2,1)} %bitcast.1, s32[4,4]{1,0:T(4,128)} %live_ref.1), custom_call_target="tpu_custom_call" | custom-call | tf_op jit(solution)/shard_map/pallas_call | solution.py:452
  79.6 2.3 %copy.4 = bf16[512,1024]{1,0:T(8,128)(2,1)} copy(bf16[512,1024]{1,0:T(8,128)(2,1)} %shard_map.28) | data formatting | bytes 2097152

commit v5 on v4

--- a/solution.py
+++ b/solution.py
@@ -10,7 +10,7 @@
 MESH = pl.DeviceIdType.MESH
 SPLIT = 2
 SUB = 2
-BEHIND = 2
+BEHIND = 1
 NT_DIMS = (((1,), (1,)), ((), ()))
 
 
@@ -207,31 +207,18 @@
     def two(at):
         return rb[pl.ds(at, 2)].reshape(2 * m, rb.shape[2])
 
-    def keep(p, q, inner, held=False):
+    def keep(p, q, inner):
         i, j = order(p), order(q)
         tile[i, j] = rn[p][:, :1] + cn[q][:1] - 2.0 * inner
 
-        @pl.when(jnp.logical_and(sent(p, q), jnp.logical_not(held)))
+        @pl.when(sent(p, q))
         def _():
             across(i, j).start()
-
-    def holds(n):
-        return jnp.logical_and(n == units - 2, inside)
-
-    def release(n):
-        i = order(n)
-
-        def one(q):
-            @pl.when(sent(n, q))
-            def _():
-                across(i, order(q)).start()
-
-        loop(n, one)
 
     def wide(n, t):
         inner = inner_of(rb[n], two(base + 2 * t))
         for j in range(2):
-            keep(n, 2 * t + j, inner[:, j * m : (j + 1) * m], holds(n))
+            keep(n, 2 * t + j, inner[:, j * m : (j + 1) * m])
 
     def tall(s, n):
         inner = inner_of(two(2 * s), rb[base + n])
@@ -330,9 +317,15 @@
         rn[n] = jnp.broadcast_to(jnp.sum(a * a, axis=1, keepdims=True), rn.shape[1:])
 
     def column_norms(n):
-        b = rb[base + n].astype(jnp.float32)
-        s = jnp.broadcast_to(jnp.sum(b * b, axis=1, keepdims=True), (m, 128))
-        cn[n] = s.T[:8]
+        @pl.when(node == 0)
+        def _():
+            cn[n] = rn[n].T[:8]
+
+        @pl.when(node != 0)
+        def _():
+            b = rb[units + n].astype(jnp.float32)
+            s = jnp.broadcast_to(jnp.sum(b * b, axis=1, keepdims=True), (m, 128))
+            cn[n] = s.T[:8]
 
     def step(n):
         gather_rows(n)
@@ -344,11 +337,7 @@
 
             @pl.when(lax.rem(n, 2) == 1)
             def _():
-                keep(n, n - 1, inner_of(rb[n], rb[base + n - 1]), holds(n))
-
-        @pl.when(holds(n - 1))
-        def _():
-            release(n - 1)
+                keep(n, n - 1, inner_of(rb[n], rb[base + n - 1]))
 
         gather_columns(n)
         column_norms(n)

time: 82.1 us -> 81.3 us (level)
  the two profiles are of different devices: /device:TPU:3 before, /device:TPU:2 now
where the time goes in v5:
time: 81.3 us; the launch traced here: 81.1 us
  Pallas kernels  78.9 us (97%)
  local copies, waits for them, and re-layouts  2.26 us (3%)
    pallas_call x1, Pallas kernels, on_device(): pl.pallas_call(functools.partial(kernel, rows, cols, lags, split, width *...  78.9 us
    unnamed x1, local copies, waits for them, and re-layouts  2.26 us

profile of v5, /device:TPU:2, one launch (start us, length us, event | category | flops | bytes accessed | tf_op | source)
XLA Modules:
  0.0 81.1 jit_solution(4537208976330789499)
XLA Ops:
  0.0 78.9 %shard_map.28 = bf16[512,1024]{1,0:T(8,128)(2,1)} custom-call(bf16[2,128,2048]{2,1,0:T(8,128)(2,1)} %bitcast.1, s32[4,4]{1,0:T(4,128)} %live_ref.1), custom_call_target="tpu_custom_call" | custom-call | tf_op jit(solution)/shard_map/pallas_call | solution.py:441
  78.9 2.3 %copy.4 = bf16[512,1024]{1,0:T(8,128)(2,1)} copy(bf16[512,1024]{1,0:T(8,128)(2,1)} %shard_map.28) | data formatting | bytes 2097152

commit v6 on v5

--- a/solution.py
+++ b/solution.py
@@ -190,8 +190,8 @@
             return c < jnp.where(jnp.logical_and(inside, a != lags - 1), cols - 2, cols - 1)
         return c > jnp.where(jnp.logical_and(inside, a != 0), 1, 0)
 
-    for side in range(2):
-        for e in range(split):
+    for e in range(split):
+        for side in range(2):
 
             @pl.when(goes_on(side, c * split + e))
             def _():
@@ -375,14 +375,19 @@
 
     lax.fori_loop(0, mine * units, landed, 0)
 
+    def put(kk):
+        rows_of = pl.ds(kk * m, m)
+        return pltpu.make_async_copy(
+            out_ref.at[rows_of], result.at[rows_of], out_sem.at[kk]
+        )
+
     def lay(kk, carry):
         for j in range(units):
             out_ref[pl.ds(kk * m, m), j * m : (j + 1) * m] = done[kk, j]
+        put(kk).start()
         return carry
 
     lax.fori_loop(0, mine, lay, 0)
-    put = pltpu.make_async_copy(out_ref, result, out_sem)
-    put.start()
 
     def drain(p, carry):
         u = order(p)
@@ -427,7 +432,7 @@
         return carry
 
     lax.fori_loop(0, mine * units, gone, 0)
-    put.wait()
+    loop(mine, lambda kk: put(kk).wait())
 
 
 def on_device(rows, cols, lags, trajectories, pair_live):
@@ -448,7 +453,7 @@
         out_specs=pl.BlockSpec(memory_space=pl.ANY),
         scratch_shapes=[
             pltpu.VMEM((mine * m, units * m), jnp.bfloat16),
-            dma,
+            dma((mine,)),
             pltpu.VMEM((2 * units, m, width), jnp.bfloat16),
             pltpu.VMEM((units, m, 128), jnp.float32),
             pltpu.VMEM((units, 8, m), jnp.float32),

time: 81.3 us -> 81.4 us (level)
  no operation moved by 1% of the time
where the time goes in v6:
time: 81.4 us; the launch traced here: 81.2 us
  Pallas kernels  78.9 us (97%)
  local copies, waits for them, and re-layouts  2.26 us (3%)
    pallas_call x1, Pallas kernels, on_device(): pl.pallas_call(functools.partial(kernel, rows, cols, lags, split, width *...  78.9 us
    unnamed x1, local copies, waits for them, and re-layouts  2.26 us

profile of v6, /device:TPU:2, one launch (start us, length us, event | category | flops | bytes accessed | tf_op | source)
XLA Modules:
  0.0 81.2 jit_solution(954030803605926756)
XLA Ops:
  0.0 78.9 %shard_map.28 = bf16[512,1024]{1,0:T(8,128)(2,1)} custom-call(bf16[2,128,2048]{2,1,0:T(8,128)(2,1)} %bitcast.1, s32[4,4]{1,0:T(4,128)} %live_ref.1), custom_call_target="tpu_custom_call" | custom-call | tf_op jit(solution)/shard_map/pallas_call | solution.py:446
  78.9 2.3 %copy.4 = bf16[512,1024]{1,0:T(8,128)(2,1)} copy(bf16[512,1024]{1,0:T(8,128)(2,1)} %shard_map.28) | data formatting | bytes 2097152
